TPU v7x, 32 devices: a whole 2x2x4 slice. The times are simulated.
32 devices in a mesh: band: 4 (over x, core), row: 8 (over z, y).
Axes of the slice: x: 2, y: 2, z: 4, core: 2. Of those that a mesh axis runs over, the one named last changes fastest.
Arguments:
- shape_coupling_matrices: bfloat16 [512, 4, 128, 128], P('row'), may hold values from 0 to 0.00390625
- target_strip_index: int32 [512, 4], P('row'), may hold values from 0 to 511, as said below
- occupied_entries_per_strip: int32 [512], P('row'), may hold values from 1 to 4
- prior_leaving_energy: bfloat16 [4, 65536], P('band', 'row'), may hold values from 0.19921875 to 3
- facet_kelvins: float32 [65536], P('row'), may hold values from 0.6 to 1.6
- emitting_ability: float32 [4, 65536], P('band', 'row'), may hold values from 0.2 to 0.9
- centre_frequency: float32 [4], P('band'), may hold values from 0.28 to 6.3
- frequency_span: float32 [4], P('band'), may hold values from 0.5 to 1.5
- prescribed_power_density: float32 [65536], P('row'), may hold values from -6 to 6
Outputs:
- corrected_kelvins: float32 [65536], P('row')
- refreshed_leaving_energy: float32 [4, 65536], P('band', 'row')
Inputs may be any that keep to these rules, and one draw needn't show every extreme that they name: `target_strip_index`: of the 256 entries of one device's rows, exactly 32 name a column tile held by each index of row.
All inputs are finite; a program needn't handle non-finite values.
Results may differ from a plain program's by a relative error of at most 0.0003.
Values may be sent and summed in bfloat16 or wider, within the bound.
No kernel may reach another device: no remote copies, remote signals or barrier semaphores. Data moves between devices by JAX's collectives and lax.ppermute only.
A program may use at most 64 MiB of HBM per device.

v0:
```python
import jax
import jax.numpy as jnp
from jax import lax
from jax.sharding import PartitionSpec as P


def emitter_terms(centre_sample, frequency_spacing, facet_kelvins):
    return (
        frequency_spacing[:, None]
        * centre_sample[:, None] ** 3
        / jnp.expm1(centre_sample[:, None] / facet_kelvins[None, :])
    )


def on_device(
    shape_coupling_matrices,
    target_strip_index,
    occupied_entries_per_strip,
    prior_leaving_energy,
    facet_kelvins,
    emitting_ability,
    centre_frequency,
    frequency_span,
    prescribed_power_density,
):
    bands_here, facets_here = prior_leaving_energy.shape
    tile_rows, slot_count = target_strip_index.shape
    tile_size = shape_coupling_matrices.shape[2]
    entries = tile_rows * slot_count
    flat_cols = target_strip_index.reshape(entries)
    gathered = lax.all_gather(prior_leaving_energy, "row", axis=1, tiled=True)
    picked = gathered.reshape(bands_here, -1, tile_size)[:, flat_cols]
    picked = picked.reshape(bands_here, tile_rows, slot_count, tile_size)
    slot_used = (
        lax.broadcasted_iota(jnp.int32, (tile_rows, slot_count), 1)
        < occupied_entries_per_strip[:, None]
    )
    masked = jnp.where(slot_used[None, :, :, None], picked, jnp.zeros_like(picked))
    incoming = jnp.einsum(
        "rkij,brkj->bri", shape_coupling_matrices, masked, preferred_element_type=jnp.float32
    ).reshape(bands_here, facets_here)
    partial_terms = emitter_terms(centre_frequency, frequency_span, facet_kelvins)
    planck_sum = lax.psum(jnp.sum(partial_terms, 0), "band")
    energy_portion = partial_terms / planck_sum
    kelvins_third_power = facet_kelvins**3
    ideal_emitter_power = energy_portion * kelvins_third_power * facet_kelvins
    refreshed_leaving_energy = (
        emitting_ability * ideal_emitter_power + (1.0 - emitting_ability) * incoming
    )
    quotient = emitting_ability / (1.0 - emitting_ability)
    flux_part = jnp.sum(quotient * (ideal_emitter_power - refreshed_leaving_energy), 0)
    gradient_piece = jnp.sum(quotient * 4.0 * energy_portion * kelvins_third_power, 0)
    balance_power_density, power_gradient = lax.psum((flux_part, gradient_piece), "band")
    corrected_kelvins = (
        facet_kelvins - (balance_power_density - prescribed_power_density) / power_gradient
    )
    return (corrected_kelvins, refreshed_leaving_energy)


def solution(mesh):
    in_specs = (
        P("row", None, None, None),
        P("row", None),
        P("row"),
        P("band", "row"),
        P("row"),
        P("band", "row"),
        P("band"),
        P("band"),
        P("row"),
    )
    out_specs = (P("row"), P("band", "row"))
    return jax.shard_map(
        on_device, mesh=mesh, in_specs=in_specs, out_specs=out_specs, check_vma=False
    )
```

profile of v0, /device:TPU:0, one launch (start us, length us, event | category | flops | bytes accessed | tf_op | source)
XLA Modules:
  0.0 104.3 jit_solution(12224050853336227778)
XLA Ops:
  7.2 0.0 copy-start
  7.2 0.0 copy-start.1
  7.2 0.0 all-reduce.3.cloned.1.call-start
  8.5 0.8 broadcast_divide_fusion
  9.3 12.9 %psum.21 = f32[8192]{0:T(1024)S(1)} all-reduce(f32[8192]{0:T(1024)S(1)} %broadcast_divide_fusion), channel_id=1, replica_groups=mesh['band'=4,'row'=8] {'band'}, use_global_device_ids=true, to_apply=%region_0.1 | all-reduce | flops 8192 | bytes 65536 | tf_op jit(solution)/shard_map/psum | solution.py:43
  22.2 31.3 %all_gather.3 = bf16[1,65536]{1,0:T(2,128)(2,1)S(1)} all-gather(bf16[1,8192]{1,0:T(2,128)(2,1)} %param.12), channel_id=1, replica_groups=mesh['band'=4,'row'=8] {'row'}, dimensions={1}, use_global_device_ids=true | all-gather | bytes 147456 | tf_op jit(solution)/shard_map/all_gather | solution.py:31
  53.5 0.8 copy.11
  54.3 0.1 reshape.85
  54.4 0.7 iota_compare_fusion
  55.1 0.8 multiply_multiply_fusion.2
  55.9 0.8 reduce
  56.7 0.9 gather_fusion
  57.6 0.1 select_bitcast_fusion
  57.7 6.3 %subtract_multiply_fusion = (f32[1,8192]{1,0:T(1,128)}, f32[1,8192]{1,0:T(1,128)S(1)}, f32[1,8192]{1,0:T(1,128)}) fusion(f32[1,8192]{1,0:T(1,128)S(1)} %bitcast.36, f32[1,8192]{1,0:T(1,128)} %param.14, bf16[64,4,128,128]{3,2,1,0:T(8,128)(2,1)} %param.9, bf16[64,4,128,1]{2,1,0,3:T(4,128)(2,1)S(1)} %select_bitcast_fusion), kind=kOutput, calls=%fused_computation.10 | convolution fusion | flops 8445952 | bytes 8617984 | tf_op jit(solution)/shard_map/rkij,brkj->bri/dot_general | solution.py:39
  64.0 0.7 multiply_multiply_fusion.1
  64.7 0.0 all-reduce.3.cloned.1.call-update
  64.7 31.3 %all-reduce.3.cloned.1.call-done = (f32[8192]{0:T(1024)}, f32[8192]{0:T(1024)}) async-done(((f32[8192]{0:T(1024)}, f32[8192]{0:T(1024)}), (f32[8192]{0:T(1024)}, f32[8192]{0:T(1024)})) %all-reduce.3.cloned.1.call-update) | async-done | bytes 65552 | tf_op jit(solution)/shard_map/psum | solution.py:53
  96.0 0.0 copy-done
  96.0 0.0 copy-done.1
  96.0 1.4 %divide_subtract_fusion = f32[8192]{0:T(1024)} fusion(f32[8192]{0:T(1024)S(1)} %copy-done, f32[8192]{0:T(1024)} %get-tuple-element.2, f32[8192]{0:T(1024)} %get-tuple-element.3, f32[8192]{0:T(1024)S(1)} %copy-done.1), kind=kLoop, calls=%fused_computation.8 | loop fusion | flops 24576 | bytes 163840 | tf_op jit(solution)/shard_map/sub | solution.py:55
  (2 shorter events, 0.0 us)
Async XLA Ops:
  7.2 88.8 %copy-start = (f32[8192]{0:T(1024)S(1)}, f32[8192]{0:T(1024)}, u32[]{:S(2)}) copy-start(f32[8192]{0:T(1024)} %param.13) | copy-start | bytes 98308
  7.2 88.8 %copy-start.1 = (f32[8192]{0:T(1024)S(1)}, f32[8192]{0:T(1024)}, u32[]{:S(2)}) copy-start(f32[8192]{0:T(1024)} %param.17) | copy-start | bytes 98308
  7.2 88.8 %all-reduce.3.cloned.1.call-start = ((), (), s32[]{:S(2)}) async-start(), calls=%async_computation | async-start | bytes 131072 | tf_op jit(solution)/shard_map/psum | solution.py:53
Sparse Core Ops, SparseCore 0:
  64.8 31.1 all-reduce.2
where the time goes:
time: 105 us; the launch traced here: 104 us
  blocking collectives  44.2 us (42%)
  waiting for transfers between devices  31.3 us (30%)
  between operations  15.4 us (15%)
  matrix products  6.3 us (6%)
  other arithmetic  5.3 us (5%)
  local copies, waits for them, and re-layouts  1.74 us (2%)
    psum x1, waiting for transfers between devices, on_device(): lax.psum((flux_part, gradient_piece), 'band')  31.3 us
    all_gather x1, blocking collectives, on_device(): gathered = lax.all_gather(prior_leaving_energy, 'row', axis=1, tiled=True)  31.3 us
    psum x1, blocking collectives, on_device(): planck_sum = lax.psum(jnp.sum(partial_terms, 0), 'band')  12.9 us
    dot_general x1, matrix products, on_device(): jnp.einsum('rkij,brkj->bri', shape_coupling_matrices, masked, preferred_e...  6.3 us
  transfers between devices with their start and end apart: 1, of which 1 were waited for; matrix products, arithmetic and copies ran while one was open for 0% of the time, Pallas kernels for 0%

commit v1 on v0

--- a/solution.py
+++ b/solution.py
@@ -28,7 +28,12 @@
     tile_size = shape_coupling_matrices.shape[2]
     entries = tile_rows * slot_count
     flat_cols = target_strip_index.reshape(entries)
-    gathered = lax.all_gather(prior_leaving_energy, "row", axis=1, tiled=True)
+    ring = [prior_leaving_energy]
+    for hop in range(7):
+        ring.append(lax.ppermute(ring[-1], "row", [(dev, (dev + 1) % 8) for dev in range(8)]))
+    gathered = jnp.roll(
+        jnp.concatenate(ring[::-1], axis=1), (lax.axis_index("row") + 1) * ring[0].shape[1], axis=1
+    )
     picked = gathered.reshape(bands_here, -1, tile_size)[:, flat_cols]
     picked = picked.reshape(bands_here, tile_rows, slot_count, tile_size)
     slot_used = (

time: 105 us -> 107 us (1.019)
  blocking collectives: 44.2 us -> 10.3 us
  waiting for transfers between devices: 31.3 us -> 62.4 us
  starting transfers between devices: 0.04 us -> 3.13 us
  local copies, waits for them, and re-layouts: 1.74 us -> 4.73 us
    ppermute x0 -> x7, waiting for transfers between devices: none -> 33.6 us  [on_device(): lax.ppermute(ring[-1], 'row', [(dev, (dev + 1) % 8) for dev in range(8)])]
    all_gather x1 -> x0, blocking collectives: 31.3 us -> none  [on_device(): gathered = lax.all_gather(prior_leaving_energy, 'row', axis=1, tiled=True)]
    ppermute x0 -> x7, starting transfers between devices: none -> 3.09 us  [on_device(): lax.ppermute(ring[-1], 'row', [(dev, (dev + 1) % 8) for dev in range(8)])]
    psum x1, blocking collectives: 12.9 us -> 10.3 us  [on_device(): planck_sum = lax.psum(jnp.sum(partial_terms, 0), 'band')]
    psum x1, waiting for transfers between devices: 31.3 us -> 28.7 us  [on_device(): lax.psum((flux_part, gradient_piece), 'band')]
    unnamed x5 -> x20, local copies, waits for them, and re-layouts: 0.78 us -> 2.22 us
  transfers between devices with their start and end apart: 1 -> 8, of which waited for: 1 -> 7; matrix products, arithmetic and copies ran while one was open for 0% -> 3% of each run, Pallas kernels for 0% -> 0%
where the time goes in v1:
time: 107 us
  waiting for transfers between devices  62.4 us (58%)
  between operations  15.4 us (14%)
  blocking collectives  10.3 us (10%)
  matrix products  6.3 us (6%)
  local copies, waits for them, and re-layouts  4.73 us (4%)
  other arithmetic  4.52 us (4%)
  starting transfers between devices  3.13 us (3%)
    ppermute x7, waiting for transfers between devices, on_device(): lax.ppermute(ring[-1], 'row', [(dev, (dev + 1) % 8) for dev in range(8)])  33.6 us
    psum x1, waiting for transfers between devices, on_device(): lax.psum((flux_part, gradient_piece), 'band')  28.7 us
    psum x1, blocking collectives, on_device(): planck_sum = lax.psum(jnp.sum(partial_terms, 0), 'band')  10.3 us
    dot_general x1, matrix products, on_device(): jnp.einsum('rkij,brkj->bri', shape_coupling_matrices, masked, preferred_e...  6.3 us
    ppermute x7, starting transfers between devices, on_device(): lax.ppermute(ring[-1], 'row', [(dev, (dev + 1) % 8) for dev in range(8)])  3.09 us
    unnamed x20, local copies, waits for them, and re-layouts  2.22 us
  transfers between devices with their start and end apart: 8, of which 7 were waited for; matrix products, arithmetic and copies ran while one was open for 3% of the time, Pallas kernels for 0%

profile of v1, /device:TPU:0, one launch (start us, length us, event | category | flops | bytes accessed | tf_op | source)
XLA Modules:
  0.0 106.8 jit_solution(1032484052199541190)
XLA Ops:
  7.2 0.0 all-reduce.3.cloned.1.call-start
  7.2 3.0 %collective-permute-start = (bf16[1,8192]{1,0:T(2,128)(2,1)}, bf16[1,8192]{1,0:T(2,128)(2,1)S(1)}, u32[]{:S(2)}, u32[]{:S(2)}) collective-permute-start(bf16[1,8192]{1,0:T(2,128)(2,1)} %param.12), channel_id=1, source_target_pairs={{0,1},{1,2},{2,3},{3,4},{4,5},{5,6},{6,7},{7,0},{8,9},{9,10},{10,1... | collective-permute-start | bytes 49160 | tf_op jit(solution)/shard_map/ppermute | solution.py:33
  11.6 3.8 %collective-permute-done = bf16[1,8192]{1,0:T(2,128)(2,1)S(1)} collective-permute-done((bf16[1,8192]{1,0:T(2,128)(2,1)}, bf16[1,8192]{1,0:T(2,128)(2,1)S(1)}, u32[]{:S(2)}, u32[]{:S(2)}) %collective-permute-start) | collective-permute-done | bytes 16416 | tf_op jit(solution)/shard_map/ppermute | solution.py:33
  15.4 0.8 broadcast_divide_fusion
  16.2 5.8 %collective-permute-done.1 = bf16[1,8192]{1,0:T(2,128)(2,1)S(1)} collective-permute-done((bf16[1,8192]{1,0:T(2,128)(2,1)S(1)}, bf16[1,8192]{1,0:T(2,128)(2,1)S(1)}, u32[]{:S(2)}, u32[]{:S(2)}) %collective-permute-start.1) | collective-permute-done | bytes 16416 | tf_op jit(solution)/shard_map/ppermute | solution.py:33
  22.0 10.3 %psum.21 = f32[8192]{0:T(1024)S(1)} all-reduce(f32[8192]{0:T(1024)S(1)} %broadcast_divide_fusion), channel_id=1, replica_groups=mesh['band'=4,'row'=8] {'band'}, use_global_device_ids=true, to_apply=%region_0.1 | all-reduce | flops 8192 | bytes 65536 | tf_op jit(solution)/shard_map/psum | solution.py:48
  32.3 0.1 collective-permute-start.3
  32.3 0.8 multiply_multiply_fusion.2
  33.1 5.8 %collective-permute-done.3 = bf16[1,8192]{1,0:T(2,128)(2,1)S(1)} collective-permute-done((bf16[1,8192]{1,0:T(2,128)(2,1)S(1)}, bf16[1,8192]{1,0:T(2,128)(2,1)S(1)}, u32[]{:S(2)}, u32[]{:S(2)}) %collective-permute-start.3) | collective-permute-done | bytes 16416 | tf_op jit(solution)/shard_map/ppermute | solution.py:33
  39.0 0.7 iota_compare_fusion
  39.7 0.8 copy.11
  40.5 0.1 reshape.85
  40.6 5.0 %collective-permute-done.4 = bf16[1,8192]{1,0:T(2,128)(2,1)S(1)} collective-permute-done((bf16[1,8192]{1,0:T(2,128)(2,1)S(1)}, bf16[1,8192]{1,0:T(2,128)(2,1)S(1)}, u32[]{:S(2)}, u32[]{:S(2)}) %collective-permute-start.4) | collective-permute-done | bytes 16416 | tf_op jit(solution)/shard_map/ppermute | solution.py:33
  45.6 6.6 %collective-permute-done.5 = bf16[1,8192]{1,0:T(2,128)(2,1)S(1)} collective-permute-done((bf16[1,8192]{1,0:T(2,128)(2,1)S(1)}, bf16[1,8192]{1,0:T(2,128)(2,1)S(1)}, u32[]{:S(2)}, u32[]{:S(2)}) %collective-permute-start.5) | collective-permute-done | bytes 16416 | tf_op jit(solution)/shard_map/ppermute | solution.py:33
  52.2 6.6 %collective-permute-done.6 = bf16[1,8192]{1,0:T(2,128)(2,1)S(1)} collective-permute-done((bf16[1,8192]{1,0:T(2,128)(2,1)S(1)}, bf16[1,8192]{1,0:T(2,128)(2,1)S(1)}, u32[]{:S(2)}, u32[]{:S(2)}) %collective-permute-start.6) | collective-permute-done | bytes 16416 | tf_op jit(solution)/shard_map/ppermute | solution.py:33
  59.1 0.8 constant_dynamic-update-slice_fusion.8
  60.2 0.8 constant_dynamic-update-slice_fusion
  61.0 0.7 dynamic-slice_reduce_fusion
  61.8 0.9 gather_fusion
  62.6 0.1 select_bitcast_fusion
  62.8 6.3 %subtract_multiply_fusion = (f32[1,8192]{1,0:T(1,128)}, f32[1,8192]{1,0:T(1,128)S(1)}, f32[1,8192]{1,0:T(1,128)}) fusion(f32[1,8192]{1,0:T(1,128)S(1)} %bitcast.36, f32[1,8192]{1,0:T(1,128)} %param.14, bf16[64,4,128,128]{3,2,1,0:T(8,128)(2,1)} %param.9, bf16[64,4,128,1]{2,1,0,3:T(4,128)(2,1)S(1)} %select_bitcast_fusion), kind=kOutput, calls=%fused_computation.27 | convolution fusion | flops 8445952 | bytes 8617984 | tf_op jit(solution)/shard_map/rkij,brkj->bri/dot_general | solution.py:44
  69.1 0.7 multiply_multiply_fusion.1
  69.8 28.7 %all-reduce.3.cloned.1.call-done = (f32[8192]{0:T(1024)}, f32[8192]{0:T(1024)}) async-done(((f32[8192]{0:T(1024)}, f32[8192]{0:T(1024)}), (f32[8192]{0:T(1024)}, f32[8192]{0:T(1024)})) %all-reduce.3.cloned.1.call-update) | async-done | bytes 65552 | tf_op jit(solution)/shard_map/psum | solution.py:58
  98.5 1.4 %divide_subtract_fusion = f32[8192]{0:T(1024)} fusion(f32[8192]{0:T(1024)S(1)} %copy-done, f32[8192]{0:T(1024)} %get-tuple-element.2, f32[8192]{0:T(1024)} %get-tuple-element.3, f32[8192]{0:T(1024)S(1)} %copy-done.1), kind=kLoop, calls=%fused_computation.25 | loop fusion | flops 24576 | bytes 163840 | tf_op jit(solution)/shard_map/sub | solution.py:60
  (27 shorter events, 0.7 us)
Async XLA Ops:
  7.2 91.3 %copy-start = (f32[8192]{0:T(1024)S(1)}, f32[8192]{0:T(1024)}, u32[]{:S(2)}) copy-start(f32[8192]{0:T(1024)} %param.13) | copy-start | bytes 98308
  7.2 91.3 %copy-start.1 = (f32[8192]{0:T(1024)S(1)}, f32[8192]{0:T(1024)}, u32[]{:S(2)}) copy-start(f32[8192]{0:T(1024)} %param.17) | copy-start | bytes 98308
  7.2 91.3 %all-reduce.3.cloned.1.call-start = ((), (), s32[]{:S(2)}) async-start(), calls=%async_computation | async-start | bytes 131072 | tf_op jit(solution)/shard_map/psum | solution.py:58
  7.2 8.2 %collective-permute-start = (bf16[1,8192]{1,0:T(2,128)(2,1)}, bf16[1,8192]{1,0:T(2,128)(2,1)S(1)}, u32[]{:S(2)}, u32[]{:S(2)}) collective-permute-start(bf16[1,8192]{1,0:T(2,128)(2,1)} %param.12), channel_id=1, source_target_pairs={{0,1},{1,2},{2,3},{3,4},{4,5},{5,6},{6,7},{7,0},{8,9},{9,10},{10,1... | collective-permute-start | bytes 49160 | tf_op jit(solution)/shard_map/ppermute | solution.py:33
  15.4 6.6 %collective-permute-start.1 = (bf16[1,8192]{1,0:T(2,128)(2,1)S(1)}, bf16[1,8192]{1,0:T(2,128)(2,1)S(1)}, u32[]{:S(2)}, u32[]{:S(2)}) collective-permute-start(bf16[1,8192]{1,0:T(2,128)(2,1)S(1)} %collective-permute-done), channel_id=1, source_target_pairs={{0,1},{1,2},{2,3},{3,4},{4,5},{5,6},{6,7},{7,0},{8,9},{9,10},{10,1... | collective-permute-start | bytes 49160 | tf_op jit(solution)/shard_map/ppermute | solution.py:33
  22.0 10.3 %collective-permute-start.2 = (bf16[1,8192]{1,0:T(2,128)(2,1)S(1)}, bf16[1,8192]{1,0:T(2,128)(2,1)S(1)}, u32[]{:S(2)}, u32[]{:S(2)}) collective-permute-start(bf16[1,8192]{1,0:T(2,128)(2,1)S(1)} %collective-permute-done.1), channel_id=1, source_target_pairs={{0,1},{1,2},{2,3},{3,4},{4,5},{5,6},{6,7},{7,0},{8,9},{9,10},{10,1... | collective-permute-start | bytes 49160 | tf_op jit(solution)/shard_map/ppermute | solution.py:33
  32.3 6.7 %collective-permute-start.3 = (bf16[1,8192]{1,0:T(2,128)(2,1)S(1)}, bf16[1,8192]{1,0:T(2,128)(2,1)S(1)}, u32[]{:S(2)}, u32[]{:S(2)}) collective-permute-start(bf16[1,8192]{1,0:T(2,128)(2,1)S(1)} %collective-permute-done.2), channel_id=1, source_target_pairs={{0,1},{1,2},{2,3},{3,4},{4,5},{5,6},{6,7},{7,0},{8,9},{9,10},{10,1... | collective-permute-start | bytes 49160 | tf_op jit(solution)/shard_map/ppermute | solution.py:33
  39.0 6.6 %collective-permute-start.4 = (bf16[1,8192]{1,0:T(2,128)(2,1)S(1)}, bf16[1,8192]{1,0:T(2,128)(2,1)S(1)}, u32[]{:S(2)}, u32[]{:S(2)}) collective-permute-start(bf16[1,8192]{1,0:T(2,128)(2,1)S(1)} %collective-permute-done.3), channel_id=1, source_target_pairs={{0,1},{1,2},{2,3},{3,4},{4,5},{5,6},{6,7},{7,0},{8,9},{9,10},{10,1... | collective-permute-start | bytes 49160 | tf_op jit(solution)/shard_map/ppermute | solution.py:33
  45.6 6.6 %collective-permute-start.5 = (bf16[1,8192]{1,0:T(2,128)(2,1)S(1)}, bf16[1,8192]{1,0:T(2,128)(2,1)S(1)}, u32[]{:S(2)}, u32[]{:S(2)}) collective-permute-start(bf16[1,8192]{1,0:T(2,128)(2,1)S(1)} %collective-permute-done.4), channel_id=1, source_target_pairs={{0,1},{1,2},{2,3},{3,4},{4,5},{5,6},{6,7},{7,0},{8,9},{9,10},{10,1... | collective-permute-start | bytes 49160 | tf_op jit(solution)/shard_map/ppermute | solution.py:33
  52.2 6.6 %collective-permute-start.6 = (bf16[1,8192]{1,0:T(2,128)(2,1)S(1)}, bf16[1,8192]{1,0:T(2,128)(2,1)S(1)}, u32[]{:S(2)}, u32[]{:S(2)}) collective-permute-start(bf16[1,8192]{1,0:T(2,128)(2,1)S(1)} %collective-permute-done.5), channel_id=1, source_target_pairs={{0,1},{1,2},{2,3},{3,4},{4,5},{5,6},{6,7},{7,0},{8,9},{9,10},{10,1... | collective-permute-start | bytes 49160 | tf_op jit(solution)/shard_map/ppermute | solution.py:33
Sparse Core Ops, SparseCore 0:
  69.9 28.5 all-reduce.2

commit v2 on v0

--- a/solution.py
+++ b/solution.py
@@ -40,7 +40,7 @@
         "rkij,brkj->bri", shape_coupling_matrices, masked, preferred_element_type=jnp.float32
     ).reshape(bands_here, facets_here)
     partial_terms = emitter_terms(centre_frequency, frequency_span, facet_kelvins)
-    planck_sum = lax.psum(jnp.sum(partial_terms, 0), "band")
+    planck_sum = jnp.sum(lax.all_gather(jnp.sum(partial_terms, 0), "band"), axis=0)
     energy_portion = partial_terms / planck_sum
     kelvins_third_power = facet_kelvins**3
     ideal_emitter_power = energy_portion * kelvins_third_power * facet_kelvins

time: 105 us -> 99.8 us (0.950)
  blocking collectives: 44.2 us -> 38.3 us
    psum x1 -> x0, blocking collectives: 12.9 us -> none  [on_device(): planck_sum = lax.psum(jnp.sum(partial_terms, 0), 'band')]
    all_gather x0 -> x1, blocking collectives: none -> 6.48 us  [on_device(): lax.all_gather(jnp.sum(partial_terms, 0), 'band')]
where the time goes in v2:
time: 99.8 us; the launch traced here: 99.3 us
  blocking collectives  38.3 us (38%)
  waiting for transfers between devices  32.1 us (32%)
  between operations  15.4 us (15%)
  matrix products  6.3 us (6%)
  other arithmetic  5.37 us (5%)
  local copies, waits for them, and re-layouts  1.79 us (2%)
    psum x1, waiting for transfers between devices, on_device(): lax.psum((flux_part, gradient_piece), 'band')  32.1 us
    all_gather x1, blocking collectives, on_device(): gathered = lax.all_gather(prior_leaving_energy, 'row', axis=1, tiled=True)  31.8 us
    all_gather x1, blocking collectives, on_device(): lax.all_gather(jnp.sum(partial_terms, 0), 'band')  6.48 us
    dot_general x1, matrix products, on_device(): jnp.einsum('rkij,brkj->bri', shape_coupling_matrices, masked, preferred_e...  6.3 us
  transfers between devices with their start and end apart: 1, of which 1 were waited for; matrix products, arithmetic and copies ran while one was open for 0% of the time, Pallas kernels for 0%

profile of v2, /device:TPU:0, one launch (start us, length us, event | category | flops | bytes accessed | tf_op | source)
XLA Modules:
  0.0 99.3 jit_solution(7757648280148859822)
XLA Ops:
  7.2 0.0 copy-start
  7.2 0.0 copy-start.1
  7.2 0.0 all-reduce.3.cloned.1.call-start
  8.5 0.8 broadcast_divide_fusion
  9.3 6.5 %all-gather = f32[32768]{0:T(1024)S(1)} all-gather(f32[8192]{0:T(1024)S(1)} %broadcast_divide_fusion), channel_id=2, replica_groups=mesh['band'=4,'row'=8] {'band'}, dimensions={0}, use_global_device_ids=true | all-gather | bytes 163840 | tf_op jit(solution)/shard_map/all_gather | solution.py:43
  15.9 31.8 %all_gather.8 = bf16[1,65536]{1,0:T(2,128)(2,1)S(1)} all-gather(bf16[1,8192]{1,0:T(2,128)(2,1)} %param.12), channel_id=1, replica_groups=mesh['band'=4,'row'=8] {'row'}, dimensions={1}, use_global_device_ids=true | all-gather | bytes 147456 | tf_op jit(solution)/shard_map/all_gather | solution.py:31
  47.7 0.8 copy.13
  48.4 0.1 reshape.85
  48.6 0.7 iota_compare_fusion
  49.3 0.1 reduce_sum.15
  49.4 0.8 multiply_multiply_fusion.2
  50.2 0.8 reduce
  51.0 0.9 gather_fusion
  51.8 0.1 select_bitcast_fusion
  52.0 6.3 %subtract_multiply_fusion = (f32[1,8192]{1,0:T(1,128)}, f32[1,8192]{1,0:T(1,128)S(1)}, f32[1,8192]{1,0:T(1,128)}) fusion(f32[1,8192]{1,0:T(1,128)S(1)} %bitcast.36, f32[1,8192]{1,0:T(1,128)} %param.14, bf16[64,4,128,128]{3,2,1,0:T(8,128)(2,1)} %param.9, bf16[64,4,128,1]{2,1,0,3:T(4,128)(2,1)S(1)} %select_bitcast_fusion), kind=kOutput, calls=%fused_computation.10 | convolution fusion | flops 8445952 | bytes 8617984 | tf_op jit(solution)/shard_map/rkij,brkj->bri/dot_general | solution.py:39
  58.3 0.7 multiply_multiply_fusion.1
  58.9 0.0 all-reduce.3.cloned.1.call-update
  59.0 32.1 %all-reduce.3.cloned.1.call-done = (f32[8192]{0:T(1024)}, f32[8192]{0:T(1024)}) async-done(((f32[8192]{0:T(1024)}, f32[8192]{0:T(1024)}), (f32[8192]{0:T(1024)}, f32[8192]{0:T(1024)})) %all-reduce.3.cloned.1.call-update) | async-done | bytes 65552 | tf_op jit(solution)/shard_map/psum | solution.py:53
  91.1 0.0 copy-done
  91.1 0.0 copy-done.1
  91.1 1.4 %divide_subtract_fusion = f32[8192]{0:T(1024)} fusion(f32[8192]{0:T(1024)S(1)} %copy-done, f32[8192]{0:T(1024)} %get-tuple-element.2, f32[8192]{0:T(1024)} %get-tuple-element.3, f32[8192]{0:T(1024)S(1)} %copy-done.1), kind=kLoop, calls=%fused_computation.8 | loop fusion | flops 24576 | bytes 163840 | tf_op jit(solution)/shard_map/sub | solution.py:55
  (3 shorter events, 0.1 us)
Async XLA Ops:
  7.2 83.9 %copy-start = (f32[8192]{0:T(1024)S(1)}, f32[8192]{0:T(1024)}, u32[]{:S(2)}) copy-start(f32[8192]{0:T(1024)} %param.13) | copy-start | bytes 98308
  7.2 83.9 %copy-start.1 = (f32[8192]{0:T(1024)S(1)}, f32[8192]{0:T(1024)}, u32[]{:S(2)}) copy-start(f32[8192]{0:T(1024)} %param.17) | copy-start | bytes 98308
  7.2 83.9 %all-reduce.3.cloned.1.call-start = ((), (), s32[]{:S(2)}) async-start(), calls=%async_computation | async-start | bytes 131072 | tf_op jit(solution)/shard_map/psum | solution.py:53
Sparse Core Ops, SparseCore 0:
  59.1 31.9 all-reduce.2
